TPU v7x, 32 devices: a whole 2x2x4 slice. The times are simulated.
32 devices in a mesh: groups: 2 (over y), expert: 4 (over x, core), hidden: 4 (over z).
Axes of the slice: x: 2, y: 2, z: 4, core: 2. Of those that a mesh axis runs over, the one named last changes fastest.
Arguments:
- tokens: bfloat16 [1024, 3072], P(('groups', 'expert'), 'hidden'), parts along dimension 0, may hold values from -6 to 6
- routes: int32 [1024, 2], P(('groups', 'expert')), parts along dimension 0, may hold values from 0 to 7, all different within a row; in each aligned block of 128 rows (0 to 127, 128 to 255, ...) at most 48 rows name the same one
- router_weight: bfloat16 [3072, 8], replicated, may hold values from -0.109375 to 0.109375
- gate_weight: bfloat16 [8, 3072, 8192], P('expert', None, 'hidden'), may hold values from -0.109375 to 0.109375
- up_weight: bfloat16 [8, 3072, 8192], P('expert', None, 'hidden'), may hold values from -0.109375 to 0.109375
- down_weight: bfloat16 [8, 8192, 3072], P('expert', 'hidden'), may hold values from -0.09375 to 0.09375
Outputs:
- mixed: bfloat16 [1024, 3072], P(('groups', 'expert'), 'hidden'), parts along dimension 0
There are 2 independent parts, one for each index of `groups`. A program takes and returns all parts, laid end to end along the dimension named above; an argument that names none is the same for every part. Nothing has to cross between parts.
Inputs may be any that keep to these rules, and one draw needn't show every extreme that they name: `routes`: each token names two different experts. Among the 128 tokens of one index of expert (aligned blocks of rows) no expert is named more than 48 times, a bound that some block reaches.
All inputs are finite; a program needn't handle non-finite values.
Results may differ from a plain program's by a relative error of at most 0.0057.
Values may be sent and summed in bfloat16 or wider, within the bound.
No kernel may reach another device: no remote copies, remote signals or barrier semaphores. Data moves between devices by JAX's collectives and lax.ppermute only.
A program may use at most 128 MiB of HBM per device.

v0:
```python
import jax
import jax.numpy as jnp
from jax import lax
from jax.sharding import PartitionSpec as P

CAP = 48


def per_device(tokens, routes, router_weight, gate_weight, up_weight, down_weight):
    experts_here = gate_weight.shape[0]
    groups = lax.axis_size("expert")
    experts_all = experts_here * groups
    local_tokens = tokens.shape[0]
    capacity = CAP
    flat_ids = routes.reshape(-1)
    onehot = (flat_ids[:, None] == jnp.arange(experts_all, dtype=jnp.int32)[None, :]).astype(
        jnp.int32
    )
    position = jnp.sum((jnp.cumsum(onehot, axis=0) - onehot) * onehot, axis=1)
    slot_of = flat_ids * capacity + position
    owners = jnp.arange(flat_ids.shape[0], dtype=jnp.int32) // 2
    inverse = jnp.full((experts_all * capacity,), local_tokens, jnp.int32).at[slot_of].set(owners)
    gathered = lax.all_gather(tokens, "hidden", axis=1, tiled=True)
    logits = jnp.dot(gathered, router_weight, preferred_element_type=jnp.float32)
    padded = jnp.concatenate([gathered, jnp.zeros((1, gathered.shape[1]), jnp.bfloat16)], axis=0)
    send_rows = padded[inverse].reshape(experts_all, 1, capacity, gathered.shape[1])
    arrived = lax.all_to_all(send_rows, "expert", split_axis=0, concat_axis=1, tiled=True)
    gate_act = jnp.einsum(
        "ensd,edf->ensf", arrived, gate_weight, preferred_element_type=jnp.float32
    )
    up_act = jnp.einsum("ensd,edf->ensf", arrived, up_weight, preferred_element_type=jnp.float32)
    hidden_act = (jax.nn.silu(gate_act) * up_act).astype(jnp.bfloat16)
    hidden_act = hidden_act.reshape(experts_here, groups * capacity, hidden_act.shape[3])
    partial_value = jnp.einsum(
        "erf,efd->erd", hidden_act, down_weight, preferred_element_type=jnp.float32
    )
    summed = lax.psum_scatter(partial_value, "hidden", scatter_dimension=2, tiled=True).astype(
        jnp.bfloat16
    )
    summed = summed.reshape(experts_here, groups, capacity, summed.shape[2])
    returned = lax.all_to_all(summed, "expert", split_axis=1, concat_axis=0, tiled=True)
    results = returned.reshape(experts_all * capacity, returned.shape[3])
    selected = jnp.take_along_axis(logits, routes, axis=1)
    share = jax.nn.sigmoid(selected[:, 0] - selected[:, 1])
    slot_pairs = slot_of.reshape(local_tokens, 2)
    first_out = results[slot_pairs[:, 0]].astype(jnp.float32)
    second_out = results[slot_pairs[:, 1]].astype(jnp.float32)
    mixture = share[:, None] * first_out + (1.0 - share)[:, None] * second_out
    return mixture.astype(jnp.bfloat16)


def solution(mesh):
    return jax.shard_map(
        per_device,
        mesh=mesh,
        in_specs=(
            P(("groups", "expert"), "hidden"),
            P(("groups", "expert"), None),
            P(),
            P("expert", None, "hidden"),
            P("expert", None, "hidden"),
            P("expert", "hidden", None),
        ),
        out_specs=P(("groups", "expert"), "hidden"),
        check_vma=False,
    )
```

profile of v0, /device:TPU:0, one launch (start us, length us, event | category | flops | bytes accessed | tf_op | source)
XLA Modules:
  0.0 209.8 jit_solution(10546477326377145028)
XLA Ops:
  6.5 0.0 copy-start
  6.5 0.0 reduce-scatter.2.cloned.1.call-start
  6.5 0.8 copy.41
  7.3 0.1 eq.29
  7.5 0.1 eq.25
  7.6 0.6 reduce-window.6
  8.2 0.2 slice_reduce_fusion
  8.5 0.1 fusion.13
  8.6 0.1 reduce_sum.15
  8.7 0.1 mul.51
  8.9 1.4 scatter_custom_fusion
  10.3 21.5 %all_gather.3 = bf16[128,3072]{1,0:T(8,128)(2,1)S(1)} all-gather(bf16[128,768]{1,0:T(8,128)(2,1)} %param.6), channel_id=1, replica_groups=mesh['groups'=2,'expert'=4,'hidden'=4] {'hidden'}, dimensions={1}, use_global_device_ids=true | all-gather | bytes 983040 | tf_op jit(solution)/shard_map/all_gather | solution.py:23
  31.8 0.0 copy-start.1
  31.8 0.9 copy-done.1
  32.7 0.1 concatenate.3
  32.8 2.9 %gather_fusion = bf16[384,3072]{1,0:T(8,128)(2,1)S(1)} fusion(bf16[129,3072]{1,0:T(8,128)(2,1)S(1)} %concatenate.3, s32[1024]{0:T(1024)S(1)} %pad_clamp_fusion.2), kind=kCustom, calls=%fused_computation | custom fusion | bytes 4720128 | tf_op jit(solution)/shard_map/gather | solution.py:26
  35.7 31.0 %all_to_all.33 = bf16[8,1,48,3072]{3,2,1,0:T(8,128)(2,1)S(1)} all-to-all(bf16[8,1,48,3072]{3,2,1,0:T(8,128)(2,1)S(1)} %bitcast.57), channel_id=1, replica_groups=mesh['groups'=2,'expert'=4,'hidden'=4] {'expert'}, dimensions={0} | all-to-all | bytes 4718592 | tf_op jit(solution)/shard_map/all_to_all | solution.py:27
  66.7 10.8 %fusion.2 = f32[2,4,48,2048]{3,2,1,0:T(8,128)S(1)} fusion(bf16[2,3072,2048]{2,1,0:T(8,128)(2,1)} %param.9, bf16[4,2,1,48,3072]{4,3,1,0,2:T(8,128)(2,1)S(1)} %bitcast.52), kind=kOutput, calls=%fused_computation.7 | convolution fusion | flops 4831838208 | bytes 30670848 | tf_op jit(solution)/shard_map/ensd,edf->ensf/dot_general | solution.py:28
  77.5 11.0 %multiply_convert_fusion = bf16[2,4,48,2048]{3,2,1,0:T(8,128)(2,1)S(1)} fusion(f32[2,4,48,2048]{3,2,1,0:T(8,128)S(1)} %fusion.2, bf16[2,3072,2048]{2,1,0:T(8,128)(2,1)} %param.10, bf16[4,2,1,48,3072]{4,3,1,0,2:T(8,128)(2,1)S(1)} %bitcast.53), kind=kOutput, calls=%fused_computation.9 | convolution fusion | flops 4836556800 | bytes 32243712 | tf_op jit(solution)/shard_map/ensd,edf->ensf/dot_general | solution.py:31
  88.5 12.9 %fusion.19 = f32[2,192,3072]{2,1,0:T(8,128)} fusion(bf16[2,192,2048]{2,1,0:T(8,128)(2,1)S(1)} %bitcast.56, bf16[2,2048,3072]{2,1,0:T(8,128)(2,1)} %param.11), kind=kOutput, calls=%fused_computation.45 | convolution fusion | flops 4831838208 | bytes 31457280 | tf_op jit(solution)/shard_map/erf,efd->erd/dot_general | solution.py:34
  101.4 0.0 copy-start.3
  101.4 0.0 copy-start.2
  101.4 0.0 reduce-scatter.2.cloned.1.call-update
  101.5 0.7 copy-done.3
  102.1 0.1 copy.39
  102.2 0.1 reshape.100
  102.4 0.0 copy-done
  102.4 0.2 copy-done.2
  102.6 0.3 fusion.18
  102.9 1.4 gather_fusion.3
  104.3 0.1 reshape.103
  104.4 0.1 copy.40
  104.5 0.2 fusion.10
  104.7 80.6 %reduce-scatter.2.cloned.1.call-done = f32[2,192,768]{2,1,0:T(8,128)} async-done(((f32[2,192,3072]{2,1,0:T(8,128)}), f32[2,192,768]{2,1,0:T(8,128)}) %reduce-scatter.2.cloned.1.call-update) | async-done | bytes 1179664 | tf_op jit(solution)/shard_map/reduce_scatter | solution.py:37
  185.3 1.3 convert_element_type.25
  186.6 0.8 copy.46
  187.5 3.5 %all-to-all-start.1 = ((bf16[2,4,48,768]{3,2,0,1:T(8,128)(2,1)}), bf16[2,4,48,768]{3,2,0,1:T(8,128)(2,1)S(1)}, u32[]{:S(2)}, u32[]{:S(2)}) async-start(bf16[2,4,48,768]{3,2,0,1:T(8,128)(2,1)} %copy.46), calls=%async_computation.2 | async-start | bytes 1179648 | tf_op jit(solution)/shard_map/all_to_all | solution.py:41
  191.0 9.5 %all-to-all-done.1 = bf16[2,4,48,768]{3,2,0,1:T(8,128)(2,1)S(1)} async-done(((bf16[2,4,48,768]{3,2,0,1:T(8,128)(2,1)}), bf16[2,4,48,768]{3,2,0,1:T(8,128)(2,1)S(1)}, u32[]{:S(2)}, u32[]{:S(2)}) %all-to-all-start.1) | async-done | bytes 589856 | tf_op jit(solution)/shard_map/all_to_all | solution.py:41
  200.4 0.9 gather_fusion.2
  201.3 0.9 gather_fusion.1
  202.2 0.8 add_convert_fusion
  (12 shorter events, 0.1 us)
Async XLA Ops:
  6.5 95.8 %copy-start = (bf16[3072,8]{0,1:T(8,128)(2,1)S(1)}, bf16[3072,8]{0,1:T(8,128)(2,1)}, u32[]{:S(2)}) copy-start(bf16[3072,8]{0,1:T(8,128)(2,1)} %param.8) | copy-start | bytes 147460
  6.5 178.8 %reduce-scatter.2.cloned.1.call-start = ((), (), s32[]{:S(2)}) async-start(), calls=%async_computation.3 | async-start | bytes 5898240 | tf_op jit(solution)/shard_map/reduce_scatter | solution.py:37
  31.8 0.9 copy-start.1
  101.4 0.7 copy-start.3
  101.4 1.1 copy-start.2
  187.5 13.0 %all-to-all-start.1 = ((bf16[2,4,48,768]{3,2,0,1:T(8,128)(2,1)}), bf16[2,4,48,768]{3,2,0,1:T(8,128)(2,1)S(1)}, u32[]{:S(2)}, u32[]{:S(2)}) async-start(bf16[2,4,48,768]{3,2,0,1:T(8,128)(2,1)} %copy.46), calls=%async_computation.2 | async-start | bytes 1179648 | tf_op jit(solution)/shard_map/all_to_all | solution.py:41
Sparse Core Ops, SparseCore 0:
  101.6 83.6 reduce-scatter.1
where the time goes:
time: 210 us
  waiting for transfers between devices  90.1 us (43%)
  blocking collectives  52.6 us (25%)
  matrix products  35 us (17%)
  between operations  13.6 us (6%)
  local copies, waits for them, and re-layouts  12.1 us (6%)
  starting transfers between devices  3.48 us (2%)
  other arithmetic  3.13 us (1%)
    reduce_scatter x1, waiting for transfers between devices, per_device(): lax.psum_scatter(partial_value, 'hidden', scatter_dimension=2, tiled=True)  80.6 us
    all_to_all x1, blocking collectives, per_device(): lax.all_to_all(send_rows, 'expert', split_axis=0, concat_axis=1, tiled=True)  31 us
    all_gather x1, blocking collectives, per_device(): gathered = lax.all_gather(tokens, 'hidden', axis=1, tiled=True)  21.5 us
    dot_general x1, matrix products, per_device(): jnp.einsum('erf,efd->erd', hidden_act, down_weight, preferred_element_typ...  12.9 us
    dot_general x1, matrix products, per_device(): jnp.einsum('ensd,edf->ensf', arrived, up_weight, preferred_element_type=j...  11 us
    dot_general x1, matrix products, per_device(): jnp.einsum('ensd,edf->ensf', arrived, gate_weight, preferred_element_type...  10.8 us
    all_to_all x1, waiting for transfers between devices, per_device(): lax.all_to_all(summed, 'expert', split_axis=1, concat_axis=0, tiled=True)  9.45 us
  transfers between devices with their start and end apart: 2, of which 2 were waited for; matrix products, arithmetic and copies ran while one was open for 1% of the time, Pallas kernels for 0%

commit v1 on v0

--- a/solution.py
+++ b/solution.py
@@ -20,7 +20,14 @@
     slot_of = flat_ids * capacity + position
     owners = jnp.arange(flat_ids.shape[0], dtype=jnp.int32) // 2
     inverse = jnp.full((experts_all * capacity,), local_tokens, jnp.int32).at[slot_of].set(owners)
-    gathered = lax.all_gather(tokens, "hidden", axis=1, tiled=True)
+    peers = lax.axis_size("hidden")
+    hops = [(i, (i + 1) % peers) for i in range(peers)]
+    parts = [tokens]
+    for far in range(1, peers):
+        parts = [lax.ppermute(parts[0], "hidden", hops), *parts]
+    whole = jnp.concatenate(parts, axis=1)
+    shift = (lax.axis_index("hidden") + 1) * parts[-1].shape[1]
+    gathered = jnp.roll(whole, shift, axis=1)
     logits = jnp.dot(gathered, router_weight, preferred_element_type=jnp.float32)
     padded = jnp.concatenate([gathered, jnp.zeros((1, gathered.shape[1]), jnp.bfloat16)], axis=0)
     send_rows = padded[inverse].reshape(experts_all, 1, capacity, gathered.shape[1])

time: 210 us -> 210 us (level)
  blocking collectives: 52.6 us -> 31 us
  waiting for transfers between devices: 90.1 us -> 108 us
  starting transfers between devices: 3.48 us -> 6.54 us
    all_gather x1 -> x0, blocking collectives: 21.5 us -> none  [per_device(): gathered = lax.all_gather(tokens, 'hidden', axis=1, tiled=True)]
    ppermute x0 -> x3, waiting for transfers between devices: none -> 18.7 us  [per_device(): parts = [lax.ppermute(parts[0], 'hidden', hops), *parts]]
    ppermute x0 -> x3, starting transfers between devices: none -> 3.06 us  [per_device(): parts = [lax.ppermute(parts[0], 'hidden', hops), *parts]]
  transfers between devices with their start and end apart: 2 -> 5, of which waited for: 2 -> 5; matrix products, arithmetic and copies ran while one was open for 1% -> 3% of each run, Pallas kernels for 0% -> 0%
where the time goes in v1:
time: 210 us
  waiting for transfers between devices  108 us (51%)
  matrix products  35 us (17%)
  blocking collectives  31 us (15%)
  between operations  13.6 us (6%)
  local copies, waits for them, and re-layouts  13.2 us (6%)
  starting transfers between devices  6.54 us (3%)
  other arithmetic  3.11 us (1%)
    reduce_scatter x1, waiting for transfers between devices, per_device(): lax.psum_scatter(partial_value, 'hidden', scatter_dimension=2, tiled=True)  79.6 us
    all_to_all x1, blocking collectives, per_device(): lax.all_to_all(send_rows, 'expert', split_axis=0, concat_axis=1, tiled=True)  31 us
    ppermute x3, waiting for transfers between devices, per_device(): parts = [lax.ppermute(parts[0], 'hidden', hops), *parts]  18.7 us
    dot_general x1, matrix products, per_device(): jnp.einsum('erf,efd->erd', hidden_act, down_weight, preferred_element_typ...  12.9 us
    dot_general x1, matrix products, per_device(): jnp.einsum('ensd,edf->ensf', arrived, up_weight, preferred_element_type=j...  10.9 us
    dot_general x1, matrix products, per_device(): jnp.einsum('ensd,edf->ensf', arrived, gate_weight, preferred_element_type...  10.8 us
    all_to_all x1, waiting for transfers between devices, per_device(): lax.all_to_all(summed, 'expert', split_axis=1, concat_axis=0, tiled=True)  9.45 us
  transfers between devices with their start and end apart: 5, of which 5 were waited for; matrix products, arithmetic and copies ran while one was open for 3% of the time, Pallas kernels for 0%

profile of v1, /device:TPU:0, one launch (start us, length us, event | category | flops | bytes accessed | tf_op | source)
XLA Modules:
  0.0 210.2 jit_solution(17007958677946700056)
XLA Ops:
  6.5 0.0 copy-start
  6.5 0.0 copy-start.3
  6.5 0.0 reduce-scatter.2.cloned.1.call-start
  6.5 3.1 %collective-permute-start = (bf16[128,768]{1,0:T(8,128)(2,1)}, bf16[128,768]{1,0:T(8,128)(2,1)S(1)}, u32[]{:S(2)}, u32[]{:S(2)}) collective-permute-start(bf16[128,768]{1,0:T(8,128)(2,1)} %param.6), channel_id=1, source_target_pairs={{0,1},{1,2},{2,3},{3,0},{4,5},{5,6},{6,7},{7,4},{8,9},{9,10},{10,1... | collective-permute-start | bytes 589832 | tf_op jit(solution)/shard_map/ppermute | solution.py:27
  9.6 0.8 copy.41
  10.4 0.1 eq.32
  10.5 0.1 eq.28
  10.7 0.6 reduce-window.6
  11.3 0.2 slice_reduce_fusion
  11.5 0.1 fusion.13
  11.6 0.1 reduce_sum.15
  11.8 0.1 mul.55
  11.9 4.8 %collective-permute-done = bf16[128,768]{1,0:T(8,128)(2,1)S(1)} collective-permute-done((bf16[128,768]{1,0:T(8,128)(2,1)}, bf16[128,768]{1,0:T(8,128)(2,1)S(1)}, u32[]{:S(2)}, u32[]{:S(2)}) %collective-permute-start) | collective-permute-done | bytes 196640 | tf_op jit(solution)/shard_map/ppermute | solution.py:27
  16.8 0.0 collective-permute-start.1
  16.8 1.4 scatter_custom_fusion
  18.2 6.5 %collective-permute-done.1 = bf16[128,768]{1,0:T(8,128)(2,1)S(1)} collective-permute-done((bf16[128,768]{1,0:T(8,128)(2,1)S(1)}, bf16[128,768]{1,0:T(8,128)(2,1)S(1)}, u32[]{:S(2)}, u32[]{:S(2)}) %collective-permute-start.1) | collective-permute-done | bytes 196640 | tf_op jit(solution)/shard_map/ppermute | solution.py:27
  24.6 0.0 collective-permute-start.2
  24.6 7.5 %collective-permute-done.2 = bf16[128,768]{1,0:T(8,128)(2,1)S(1)} collective-permute-done((bf16[128,768]{1,0:T(8,128)(2,1)S(1)}, bf16[128,768]{1,0:T(8,128)(2,1)S(1)}, u32[]{:S(2)}, u32[]{:S(2)}) %collective-permute-start.2) | collective-permute-done | bytes 196640 | tf_op jit(solution)/shard_map/ppermute | solution.py:27
  32.2 0.9 constant_dynamic-update-slice_fusion.4
  33.2 0.0 copy-done.3
  33.2 0.3 constant_dynamic-slice_fusion
  33.5 0.0 copy-start.1
  33.5 0.9 copy-done.1
  34.4 0.1 concatenate.10
  34.5 2.9 %gather_fusion = bf16[384,3072]{1,0:T(8,128)(2,1)S(1)} fusion(bf16[129,3072]{1,0:T(8,128)(2,1)S(1)} %concatenate.10, s32[1024]{0:T(1024)S(1)} %pad_clamp_fusion.2), kind=kCustom, calls=%fused_computation | custom fusion | bytes 4720128 | tf_op jit(solution)/shard_map/gather | solution.py:33
  37.4 31.0 %all_to_all.33 = bf16[8,1,48,3072]{3,2,1,0:T(8,128)(2,1)S(1)} all-to-all(bf16[8,1,48,3072]{3,2,1,0:T(8,128)(2,1)S(1)} %bitcast.57), channel_id=1, replica_groups=mesh['groups'=2,'expert'=4,'hidden'=4] {'expert'}, dimensions={0} | all-to-all | bytes 4718592 | tf_op jit(solution)/shard_map/all_to_all | solution.py:34
  68.3 10.8 %fusion.2 = f32[2,4,48,2048]{3,2,1,0:T(8,128)S(1)} fusion(bf16[2,3072,2048]{2,1,0:T(8,128)(2,1)} %param.9, bf16[4,2,1,48,3072]{4,3,1,0,2:T(8,128)(2,1)S(1)} %bitcast.52), kind=kOutput, calls=%fused_computation.7 | convolution fusion | flops 4831838208 | bytes 30670848 | tf_op jit(solution)/shard_map/ensd,edf->ensf/dot_general | solution.py:35
  79.1 10.9 %multiply_convert_fusion = bf16[2,4,48,2048]{3,2,1,0:T(8,128)(2,1)S(1)} fusion(f32[2,4,48,2048]{3,2,1,0:T(8,128)S(1)} %fusion.2, bf16[2,3072,2048]{2,1,0:T(8,128)(2,1)} %param.10, bf16[4,2,1,48,3072]{4,3,1,0,2:T(8,128)(2,1)S(1)} %bitcast.53), kind=kOutput, calls=%fused_computation.9 | convolution fusion | flops 4836556800 | bytes 32243712 | tf_op jit(solution)/shard_map/ensd,edf->ensf/dot_general | solution.py:38
  90.1 12.9 %fusion.19 = f32[2,192,3072]{2,1,0:T(8,128)} fusion(bf16[2,192,2048]{2,1,0:T(8,128)(2,1)S(1)} %bitcast.56, bf16[2,2048,3072]{2,1,0:T(8,128)(2,1)} %param.11), kind=kOutput, calls=%fused_computation.54 | convolution fusion | flops 4831838208 | bytes 31457280 | tf_op jit(solution)/shard_map/erf,efd->erd/dot_general | solution.py:41
  103.0 0.0 reduce-scatter.2.cloned.1.call-update
  103.0 0.7 copy-done.4
  103.7 0.1 copy.39
  103.8 0.1 reshape.100
  104.0 0.2 fusion.10
  104.2 0.0 copy-done
  104.2 0.0 copy-done.2
  104.2 0.3 fusion.18
  104.5 1.4 gather_fusion.3
  105.9 0.1 reshape.103
  106.0 0.1 copy.40
  106.1 79.6 %reduce-scatter.2.cloned.1.call-done = f32[2,192,768]{2,1,0:T(8,128)} async-done(((f32[2,192,3072]{2,1,0:T(8,128)}), f32[2,192,768]{2,1,0:T(8,128)}) %reduce-scatter.2.cloned.1.call-update) | async-done | bytes 1179664 | tf_op jit(solution)/shard_map/reduce_scatter | solution.py:44
  185.6 1.3 convert_element_type.25
  187.0 0.8 copy.46
  187.8 3.5 %all-to-all-start.1 = ((bf16[2,4,48,768]{3,2,0,1:T(8,128)(2,1)}), bf16[2,4,48,768]{3,2,0,1:T(8,128)(2,1)S(1)}, u32[]{:S(2)}, u32[]{:S(2)}) async-start(bf16[2,4,48,768]{3,2,0,1:T(8,128)(2,1)} %copy.46), calls=%async_computation.2 | async-start | bytes 1179648 | tf_op jit(solution)/shard_map/all_to_all | solution.py:48
  191.3 9.5 %all-to-all-done.1 = bf16[2,4,48,768]{3,2,0,1:T(8,128)(2,1)S(1)} async-done(((bf16[2,4,48,768]{3,2,0,1:T(8,128)(2,1)}), bf16[2,4,48,768]{3,2,0,1:T(8,128)(2,1)S(1)}, u32[]{:S(2)}, u32[]{:S(2)}) %all-to-all-start.1) | async-done | bytes 589856 | tf_op jit(solution)/shard_map/all_to_all | solution.py:48
  200.8 0.9 gather_fusion.2
  201.7 0.9 gather_fusion.1
  202.5 0.8 add_convert_fusion
  (21 shorter events, 0.2 us)
Async XLA Ops:
  6.5 97.6 %copy-start = (bf16[3072,8]{0,1:T(8,128)(2,1)S(1)}, bf16[3072,8]{0,1:T(8,128)(2,1)}, u32[]{:S(2)}) copy-start(bf16[3072,8]{0,1:T(8,128)(2,1)} %param.8) | copy-start | bytes 147460
  6.5 26.6 %copy-start.3 = (bf16[128,768]{1,0:T(8,128)(2,1)S(1)}, bf16[128,768]{1,0:T(8,128)(2,1)}, u32[]{:S(2)}) copy-start(bf16[128,768]{1,0:T(8,128)(2,1)} %param.6) | copy-start | bytes 589828
  6.5 179.1 %reduce-scatter.2.cloned.1.call-start = ((), (), s32[]{:S(2)}) async-start(), calls=%async_computation.3 | async-start | bytes 5898240 | tf_op jit(solution)/shard_map/reduce_scatter | solution.py:44
  6.5 10.2 %collective-permute-start = (bf16[128,768]{1,0:T(8,128)(2,1)}, bf16[128,768]{1,0:T(8,128)(2,1)S(1)}, u32[]{:S(2)}, u32[]{:S(2)}) collective-permute-start(bf16[128,768]{1,0:T(8,128)(2,1)} %param.6), channel_id=1, source_target_pairs={{0,1},{1,2},{2,3},{3,0},{4,5},{5,6},{6,7},{7,4},{8,9},{9,10},{10,1... | collective-permute-start | bytes 589832 | tf_op jit(solution)/shard_map/ppermute | solution.py:27
  16.8 7.9 %collective-permute-start.1 = (bf16[128,768]{1,0:T(8,128)(2,1)S(1)}, bf16[128,768]{1,0:T(8,128)(2,1)S(1)}, u32[]{:S(2)}, u32[]{:S(2)}) collective-permute-start(bf16[128,768]{1,0:T(8,128)(2,1)S(1)} %collective-permute-done), channel_id=1, source_target_pairs={{0,1},{1,2},{2,3},{3,0},{4,5},{5,6},{6,7},{7,4},{8,9},{9,10},{10,1... | collective-permute-start | bytes 589832 | tf_op jit(solution)/shard_map/ppermute | solution.py:27
  24.6 7.5 %collective-permute-start.2 = (bf16[128,768]{1,0:T(8,128)(2,1)S(1)}, bf16[128,768]{1,0:T(8,128)(2,1)S(1)}, u32[]{:S(2)}, u32[]{:S(2)}) collective-permute-start(bf16[128,768]{1,0:T(8,128)(2,1)S(1)} %collective-permute-done.1), channel_id=1, source_target_pairs={{0,1},{1,2},{2,3},{3,0},{4,5},{5,6},{6,7},{7,4},{8,9},{9,10},{10,1... | collective-permute-start | bytes 589832 | tf_op jit(solution)/shard_map/ppermute | solution.py:27
  33.5 0.9 copy-start.1
  103.0 0.7 copy-start.4
  103.0 1.2 copy-start.2
  187.8 13.0 %all-to-all-start.1 = ((bf16[2,4,48,768]{3,2,0,1:T(8,128)(2,1)}), bf16[2,4,48,768]{3,2,0,1:T(8,128)(2,1)S(1)}, u32[]{:S(2)}, u32[]{:S(2)}) async-start(bf16[2,4,48,768]{3,2,0,1:T(8,128)(2,1)} %copy.46), calls=%async_computation.2 | async-start | bytes 1179648 | tf_op jit(solution)/shard_map/all_to_all | solution.py:48
Sparse Core Ops, SparseCore 0:
  103.2 82.4 reduce-scatter.1
